TPU v7x, 512 devices: a whole 4x4x16 slice. The times are simulated.
512 devices in a mesh: layer: 8 (over x, core), example: 64 (over z, y).
Axes of the slice: x: 4, y: 4, z: 16, core: 2. Of those that a mesh axis runs over, the one named last changes fastest.
Arguments:
- adapter_input: bfloat16 [8, 8, 262144], P('layer', None, 'example'), may hold values from -4 to 4
- output_gradient: bfloat16 [8, 262144, 512], P('layer', 'example'), may hold values from -4 to 4
- projection: bfloat16 [8, 4, 512, 128], P('layer'), may hold values from -0.25 to 0.25
- input_block_index: int32 [8, 4, 4], P('layer'), may hold values from 0 to 31
- turn_token_length: int32 [8192], P('example'), may hold values from 1 to 32, as said below
- turn_to_example: int32 [8192], P('example'), may hold values from 0 to 4095, as said below
Outputs:
- factor: float32 [512, 512], P('example')
- whitened: float32 [4096, 512], P(('example', 'layer'))
Inputs may be any that keep to these rules, and one draw needn't show every extreme that they name: `turn_token_length`: within each shard of 128 turns the lengths add up to at most 4096. `turn_to_example`: the turns of shard s carry the example numbers s * 64 to (s + 1) * 64 - 1, never falling, each at least once.
All inputs are finite; a program needn't handle non-finite values.
Results may differ from a plain program's by a relative error of at most 0.0033.
Values sent between devices are 32-bit elements; how exact they have to be, the bound alone decides.
No kernel may reach another device: no remote copies, remote signals or barrier semaphores. Data moves between devices by JAX's collectives and lax.ppermute only.
A program may use at most 64 MiB of HBM per device.

v0:
```python
import math

import jax
import jax.numpy as jnp
from jax import lax
from jax.sharding import PartitionSpec as P

EX_DEV = 64


def shards(
    adapter_input,
    output_gradient,
    projection,
    input_block_index,
    turn_token_length,
    turn_to_example,
):
    adapter_rows = adapter_input[0]
    grad_rows = output_gradient[0]
    proj_blocks = projection[0]
    picked = input_block_index[0]
    adapter_rank = adapter_rows.shape[0]
    count_of_tokens = grad_rows.shape[0]
    key_value_width = grad_rows.shape[1]
    shard_count = lax.axis_size("example")
    shard_owned_rows = EX_DEV // lax.axis_size("layer")
    owners = turn_to_example - lax.axis_index("example") * EX_DEV
    turn_ends = jnp.cumsum(turn_token_length)
    starts = turn_ends - turn_token_length
    position = jnp.arange(count_of_tokens, dtype=jnp.int32)
    inside = (
        (position[None, :] >= starts[:, None]) & (position[None, :] < turn_ends[:, None])
    ).astype(jnp.bfloat16)
    member = (owners[None, :] == jnp.arange(EX_DEV, dtype=jnp.int32)[:, None]).astype(jnp.bfloat16)
    ownership_mask = jnp.dot(member, inside, preferred_element_type=jnp.float32).astype(
        jnp.bfloat16
    )
    weighted_rows = (ownership_mask[:, None, :] * adapter_rows[None, :, :]).reshape(
        shard_owned_rows * lax.axis_size("layer") * adapter_rank, count_of_tokens
    )
    summed_total = jnp.dot(weighted_rows, grad_rows, preferred_element_type=jnp.float32)
    gradient_value = summed_total.reshape(
        shard_owned_rows * lax.axis_size("layer"), adapter_rank * key_value_width
    ).astype(jnp.bfloat16)
    pieces = []
    for column in range(proj_blocks.shape[0]):
        chosen = jnp.concatenate(
            [
                lax.dynamic_slice_in_dim(gradient_value, picked[column, slot_index] * 128, 128, 1)
                for slot_index in range(picked.shape[1])
            ],
            axis=1,
        )
        pieces.append(jnp.dot(chosen, proj_blocks[column], preferred_element_type=jnp.float32))
    features = lax.psum_scatter(
        jnp.concatenate(pieces, axis=1), "layer", scatter_dimension=0, tiled=True
    )
    local_gram = jnp.dot(
        features.T, features, precision=lax.Precision.HIGHEST, preferred_element_type=jnp.float32
    )
    gram_matrix = lax.psum(local_gram, ("layer", "example"))
    lower_factor = jnp.linalg.cholesky(gram_matrix)
    scale = math.sqrt(EX_DEV * shard_count)
    side_rows = gram_matrix.shape[0] // shard_count
    band = (
        lax.dynamic_slice_in_dim(
            lower_factor.T, lax.axis_index("example") * side_rows, side_rows, 0
        )
        / scale
    )
    whitened = jax.scipy.linalg.solve_triangular(lower_factor, features.T, lower=True).T * scale
    return (band, whitened)


def solution(mesh):
    in_specs = (
        P("layer", None, "example"),
        P("layer", "example", None),
        P("layer", None, None, None),
        P("layer", None, None),
        P("example"),
        P("example"),
    )
    out_specs = (P("example", None), P(("example", "layer"), None))
    return jax.shard_map(shards, mesh=mesh, in_specs=in_specs, out_specs=out_specs, check_vma=False)
```

profile of v0, /device:TPU:1, one launch (start us, length us, event | category | flops | bytes accessed | tf_op | source)
XLA Modules:
  0.0 695.0 jit_solution(3721714853136063381)
XLA Ops:
  7.2 2.0 fusion.93
  19.3 0.8 copy.15
  20.3 0.7 sub.11
  21.0 0.7 broadcast_subtract_fusion
  21.6 0.7 convolution_convert_fusion
  22.4 4.6 fusion.8
  28.1 0.7 pad_maximum_fusion
  29.1 42.1 %reduce-scatter.2.cloned.1.call-done = f32[8,512]{1,0:T(8,128)} async-done(((f32[64,512]{1,0:T(8,128)}), f32[8,512]{1,0:T(8,128)}) %reduce-scatter.2.cloned.1.call-update) | async-done | bytes 16400 | tf_op jit(solution)/shard_map/reduce_scatter | solution.py:56
  71.2 2.8 fusion.94
  74.1 476.2 %all-reduce.3.cloned.1.call-done = f32[512,512]{0,1:T(8,128)} async-done(((f32[512,512]{0,1:T(8,128)}), f32[512,512]{0,1:T(8,128)}) %all-reduce.3.cloned.1.call-update) | async-done | bytes 1048592 | tf_op jit(solution)/shard_map/psum | solution.py:62
  550.3 1.6 copy.17
  551.9 1.4 fusion.13
  553.4 11.7 %cholesky.104 = f32[128,128]{1,0:T(8,128)S(1)} custom-call(f32[128,128]{1,0:T(8,128)S(1)} %cholesky.266), custom_call_target="Cholesky" | custom-call | tf_op jit(solution)/shard_map/jit(cholesky)/cholesky | solution.py:63
  565.1 9.8 %custom-call.31 = f32[1,128,128]{1,2,0:T(8,128)S(1)} custom-call(f32[1,128,128]{2,1,0:T(8,128)S(1)} %get-tuple-element.51), custom_call_target="InvertDiagBlocksLowerTriangular" | custom-call | tf_op jit(solution)/shard_map/jit(cholesky)/cholesky | solution.py:63
  576.1 11.7 %cholesky.217 = f32[128,128]{1,0:T(8,128)S(1)} custom-call(f32[128,128]{1,0:T(8,128)S(1)} %cholesky.270), custom_call_target="Cholesky" | custom-call | tf_op jit(solution)/shard_map/jit(cholesky)/cholesky | solution.py:63
  587.9 9.9 %custom-call.32 = f32[1,128,128]{1,2,0:T(8,128)S(1)} custom-call(f32[1,128,128]{2,1,0:T(8,128)S(1)} %get-tuple-element.48), custom_call_target="InvertDiagBlocksLowerTriangular" | custom-call | tf_op jit(solution)/shard_map/jit(cholesky)/cholesky | solution.py:63
  598.5 11.7 %cholesky.238 = f32[128,128]{1,0:T(8,128)S(1)} custom-call(f32[128,128]{1,0:T(8,128)S(1)} %cholesky.275), custom_call_target="Cholesky" | custom-call | tf_op jit(solution)/shard_map/jit(cholesky)/cholesky | solution.py:63
  610.2 0.7 compare_reduce_fusion.1
  610.9 9.8 %custom-call.33 = f32[1,128,128]{1,2,0:T(8,128)S(1)} custom-call(f32[1,128,128]{2,1,0:T(8,128)S(1)} %get-tuple-element.45), custom_call_target="InvertDiagBlocksLowerTriangular" | custom-call | tf_op jit(solution)/shard_map/jit(cholesky)/cholesky | solution.py:63
  621.3 11.9 %cholesky.255 = f32[128,128]{1,0:T(8,128)S(1)} custom-call(f32[128,128]{1,0:T(8,128)S(1)} %convolution_subtract_fusion.2), custom_call_target="Cholesky" | custom-call | tf_op jit(solution)/shard_map/jit(cholesky)/cholesky | solution.py:63
  633.3 0.6 compare_reduce_fusion
  633.9 0.7 compare_reduce_fusion.2
  637.4 8.5 %while.1 = (s32[]{:T(128)}, f32[512,512]{1,0:T(8,128)S(1)}, s32[4,2]{0,1:T(2,128)S(1)}, f32[4,128,128]{2,1,0:T(8,128)S(1)}, s32[]{:T(128)}) while((s32[]{:T(128)}, f32[512,512]{1,0:T(8,128)S(1)}, s32[4,2]{0,1:T(2,128)S(1)}, f32[4,128,128]{2,1,0:T(8,128)S(1)}, s32[]{:T(128)}) %tuple.63), condition=%wide.while_cond, body=%wide.while_body.sunk | while | flops 2 | bytes 131181 | solution.py:72
  637.5 0.6 fusion.103
  638.1 1.4 bitcast_dynamic-update-slice_fusion.2
  639.6 0.6 fusion.103
  640.2 1.4 bitcast_dynamic-update-slice_fusion.2
  642.3 1.4 bitcast_dynamic-update-slice_fusion.2
  644.5 1.4 bitcast_dynamic-update-slice_fusion.2
  645.9 39.3 %custom-call.34 = f32[4,128,128]{1,2,0:T(8,128)S(1)} custom-call(f32[4,128,128]{2,1,0:T(8,128)S(1)} %get-tuple-element.9), custom_call_target="InvertDiagBlocksLowerTriangular" | custom-call | tf_op jit(solution)/shard_map/jit(_solve_triangular)/triangular_solve | solution.py:72
  686.7 0.6 fusion.75
  687.5 0.7 copy.21
  (50 shorter events, 7.5 us)
Async XLA Ops:
  7.2 64.0 %reduce-scatter.2.cloned.1.call-start = ((), (), s32[]{:S(2)}) async-start(), calls=%async_computation.1 | async-start | bytes 147456 | tf_op jit(solution)/shard_map/reduce_scatter | solution.py:56
  22.4 5.1 copy-start.1
  28.8 521.5 %all-reduce.3.cloned.1.call-start = ((), (), s32[]{:S(2)}) async-start(), calls=%async_computation.2 | async-start | bytes 2097152 | tf_op jit(solution)/shard_map/psum | solution.py:62
  575.5 109.8 %copy-start = (f32[8,512]{1,0:T(8,128)S(1)}, f32[8,512]{1,0:T(8,128)}, u32[]{:S(2)}) copy-start(f32[8,512]{1,0:T(8,128)} %reduce-scatter.2.cloned.1.call-done) | copy-start | bytes 49156
Sparse Core Ops, SparseCore 0:
  28.9 42.1 reduce-scatter.1
  76.6 473.6 all-reduce.2
where the time goes:
time: 696 us; the launch traced here: 695 us
  waiting for transfers between devices  518 us (74%)
  other arithmetic  123 us (18%)
  between operations  27 us (4%)
  local copies, waits for them, and re-layouts  14.1 us (2%)
  matrix products  12.4 us (2%)
    psum x1, waiting for transfers between devices, shards(): gram_matrix = lax.psum(local_gram, ('layer', 'example'))  476 us
    another operation x14, other arithmetic, shards(): lower_factor = jnp.linalg.cholesky(gram_matrix)  78.7 us
    reduce_scatter x1, waiting for transfers between devices, shards(): lax.psum_scatter(jnp.concatenate(pieces, axis=1), 'layer', scatter_dimens...  42.1 us
    another operation x3, other arithmetic, shards(): jax.scipy.linalg.solve_triangular(lower_factor, features.T, lower=True)  39.6 us
  transfers between devices with their start and end apart: 2, of which 2 were waited for; matrix products, arithmetic and copies ran while one was open for 0% of the time, Pallas kernels for 0%

commit v1 on v0

v1 whole, which is shorter than its diff:
```python
import functools
import math

import jax
import jax.numpy as jnp
from jax import lax
from jax.experimental import pallas as pl
from jax.experimental.pallas import tpu as pltpu
from jax.sharding import Mesh
from jax.sharding import PartitionSpec as P

EX_DEV = 64
HI=lax.Precision.HIGHEST
B=128; S=8
def lane_b(x,l): return jnp.broadcast_to(x[:,l:l+1],x.shape)
def sub_b(x,i): return jnp.broadcast_to(x[i:i+1,:],x.shape)
def dot(a,b,ca,cb):
    return lax.dot_general(a,b,(((ca,),(cb,)),((),())),precision=HI,preferred_element_type=jnp.float32)
def factor_block(a_ref, off, u_out, i_out):
    n=B//S
    rows=[a_ref[pl.ds(off+S*g,S),pl.ds(off,B)] for g in range(n)]
    lane=lax.broadcasted_iota(jnp.int32,(S,B),1); sub=lax.broadcasted_iota(jnp.int32,(S,B),0)
    inv=[(lane==sub+S*g).astype(jnp.float32) for g in range(n)]
    for s in range(n):
        cols=[[lane_b(rows[g],S*s+k) for k in range(S)] for g in range(s,n)]
        a=[[sub_b(cols[0][k],i) if i>=k else None for k in range(S)] for i in range(S)]
        low=[[None]*S for _ in range(S)]; d=[None]*S
        ru=[None]*S; ri=[None]*S
        for k in range(S):
            d[k]=lax.rsqrt(a[k][k])
            for i in range(k+1,S): low[i][k]=a[i][k]*d[k]
            for i in range(k+1,S):
                for j in range(k+1,i+1): a[i][j]=a[i][j]-low[i][k]*low[j][k]
            pu=sub_b(rows[s],k); pi=sub_b(inv[s],k)
            for m in range(k):
                pu=pu-low[k][m]*ru[m]; pi=pi-low[k][m]*ri[m]
            ru[k]=pu*d[k]; ri[k]=pi*d[k]
        for g in range(s+1,n):
            c=cols[g-s]; lc=[None]*S
            for k in range(S):
                v=c[k]
                for m in range(k): v=v-low[k][m]*lc[m]
                lc[k]=v*d[k]
            for k in range(S):
                rows[g]=rows[g]-lc[k]*ru[k]; inv[g]=inv[g]-lc[k]*ri[k]
        u=ru[0]; v=ri[0]
        for k in range(1,S):
            u=jnp.where(sub==k,ru[k],u); v=jnp.where(sub==k,ri[k],v)
        u_out[pl.ds(S*s,S),:]=u; i_out[pl.ds(S*s,S),:]=v
def factor_kernel(scale,shard_ref,g_ref,f_ref,band_ref,w_ref,a,u,linv,ublk,fs):
    n=g_ref.shape[0]; nb=n//B
    a[...]=g_ref[...]
    fs[...]=f_ref[...]
    def body(kb,_):
        off=pl.multiple_of(kb*B,B)
        factor_block(a,off,ublk,linv)
        r=lax.broadcasted_iota(jnp.int32,(B,B),0); c=lax.broadcasted_iota(jnp.int32,(B,B),1)
        u[pl.ds(off,B),pl.ds(off,B)]=jnp.where(c>=r,ublk[...],0.0)
        for kk in range(nb):
            @pl.when(kb==kk)
            def _():
                lo=kk*B; hi=lo+B
                li=linv[...]
                w=dot(fs[:,lo:hi],li,1,1)
                w_ref[:,lo:hi]=w*scale
                if hi<n:
                    p=dot(li,a[lo:hi,hi:],1,0)
                    u[lo:hi,hi:]=p
                    fs[:,hi:]=fs[:,hi:]-dot(w,p,1,0)
                    for ib in range(kk+1,nb):
                        q=(ib-kk-1)*B
                        a[ib*B:(ib+1)*B,ib*B:]=a[ib*B:(ib+1)*B,ib*B:]-dot(p[:,q:q+B],p[:,q:],0,0)
        return 0
    lax.fori_loop(0,nb,body,0)
    rows=band_ref.shape[0]
    start=pl.multiple_of(shard_ref[0]*rows,rows)
    x=u[pl.ds(start,rows),:]
    r=lax.broadcasted_iota(jnp.int32,x.shape,0)+start; c=lax.broadcasted_iota(jnp.int32,x.shape,1)
    band_ref[...]=jnp.where(c>=r,x,0.0)/scale

def factor_and_whiten(gram, features, shard, scale, side_rows):
    n = gram.shape[0]
    return pl.pallas_call(
        functools.partial(factor_kernel, scale),
        out_shape=(
            jax.ShapeDtypeStruct((side_rows, n), jnp.float32),
            jax.ShapeDtypeStruct(features.shape, jnp.float32),
        ),
        in_specs=[
            pl.BlockSpec(memory_space=pltpu.SMEM),
            pl.BlockSpec(memory_space=pltpu.VMEM),
            pl.BlockSpec(memory_space=pltpu.VMEM),
        ],
        out_specs=[pl.BlockSpec(memory_space=pltpu.VMEM)] * 2,
        scratch_shapes=[
            pltpu.VMEM((n, n), jnp.float32),
            pltpu.VMEM((n, n), jnp.float32),
            pltpu.VMEM((B, B), jnp.float32),
            pltpu.VMEM((B, B), jnp.float32),
            pltpu.VMEM(features.shape, jnp.float32),
        ],
        name="factor_whiten",
    )(shard, gram, features)


def shards(
    adapter_input,
    output_gradient,
    projection,
    input_block_index,
    turn_token_length,
    turn_to_example,
):
    adapter_rows = adapter_input[0]
    grad_rows = output_gradient[0]
    proj_blocks = projection[0]
    picked = input_block_index[0]
    adapter_rank = adapter_rows.shape[0]
    count_of_tokens = grad_rows.shape[0]
    key_value_width = grad_rows.shape[1]
    layers = lax.axis_size("layer")
    z_size = lax.axis_size("z")
    y_size = lax.axis_size("y")
    shard_count = z_size * y_size
    shard = lax.axis_index("z") * y_size + lax.axis_index("y")
    owners = turn_to_example - shard * EX_DEV
    turn_ends = jnp.cumsum(turn_token_length)
    starts = turn_ends - turn_token_length
    position = jnp.arange(count_of_tokens, dtype=jnp.int32)
    inside = (
        (position[None, :] >= starts[:, None]) & (position[None, :] < turn_ends[:, None])
    ).astype(jnp.bfloat16)
    member = (owners[None, :] == jnp.arange(EX_DEV, dtype=jnp.int32)[:, None]).astype(jnp.bfloat16)
    ownership_mask = jnp.dot(member, inside, preferred_element_type=jnp.float32).astype(
        jnp.bfloat16
    )
    weighted_rows = (ownership_mask[:, None, :] * adapter_rows[None, :, :]).reshape(
        EX_DEV * adapter_rank, count_of_tokens
    )
    summed_total = jnp.dot(weighted_rows, grad_rows, preferred_element_type=jnp.float32)
    gradient_value = summed_total.reshape(EX_DEV, adapter_rank * key_value_width).astype(
        jnp.bfloat16
    )
    pieces = []
    for column in range(proj_blocks.shape[0]):
        chosen = jnp.concatenate(
            [
                lax.dynamic_slice_in_dim(gradient_value, picked[column, slot_index] * 128, 128, 1)
                for slot_index in range(picked.shape[1])
            ],
            axis=1,
        )
        pieces.append(jnp.dot(chosen, proj_blocks[column], preferred_element_type=jnp.float32))
    partial = jnp.concatenate(pieces, axis=1)
    width = partial.shape[1]
    own_rows = EX_DEV // layers
    by_layer = lax.all_to_all(partial.reshape(layers, own_rows, width), "layer", 0, 0)
    features = jnp.sum(by_layer, axis=0)
    group = layers * y_size
    plane = lax.all_to_all(
        jnp.broadcast_to(features[None], (group, own_rows, width)), ("layer", "y"), 0, 0
    ).reshape(group * own_rows, width)
    mine = lax.axis_index("layer") * y_size + lax.axis_index("y")
    slab = width // group
    columns = lax.dynamic_slice_in_dim(plane, mine * slab, slab, 1)
    gram_part = jnp.dot(
        columns.T, plane, precision=lax.Precision.HIGHEST, preferred_element_type=jnp.float32
    )
    lanes = 128
    by_z = lax.all_to_all(gram_part.reshape(z_size, (slab // z_size) * width // lanes, lanes), "z", 0, 0)
    gram_row = jnp.sum(by_z, axis=0)
    gram_slab = lax.all_to_all(jnp.broadcast_to(gram_row[None], by_z.shape), "z", 0, 0)
    gram_slab = gram_slab.reshape(slab * width // lanes, lanes)
    gram_matrix = lax.all_to_all(
        jnp.broadcast_to(gram_slab[None], (group,) + gram_slab.shape), ("layer", "y"), 0, 0
    ).reshape(width, width)
    scale = math.sqrt(EX_DEV * shard_count)
    band, whitened = factor_and_whiten(
        gram_matrix, features, shard[None].astype(jnp.int32), scale, width // shard_count
    )
    return (band, whitened)


def solution(mesh):
    layer_count, shard_count = mesh.devices.shape
    y_size = 4
    fine = Mesh(
        mesh.devices.reshape(layer_count, shard_count // y_size, y_size), ("layer", "z", "y")
    )
    in_specs = (
        P("layer", None, ("z", "y")),
        P("layer", ("z", "y"), None),
        P("layer", None, None, None),
        P("layer", None, None),
        P(("z", "y")),
        P(("z", "y")),
    )
    out_specs = (P(("z", "y"), None), P(("z", "y", "layer"), None))
    return jax.shard_map(shards, mesh=fine, in_specs=in_specs, out_specs=out_specs, check_vma=False)
```

time: 696 us -> 139 us (0.20)
  waiting for transfers between devices: 518 us -> 11.2 us
  other arithmetic: 123 us -> 1.65 us
  blocking collectives: 0 us -> 75.7 us
  Pallas kernels: 0 us -> 22.6 us
  between operations: 27 us -> 10.8 us
  local copies, waits for them, and re-layouts: 14.1 us -> 5.46 us
    psum x1 -> x0, waiting for transfers between devices: 476 us -> none  [shards(): gram_matrix = lax.psum(local_gram, ('layer', 'example'))]
    another operation x19 -> x2, other arithmetic: 119 us -> 0.27 us  [the longest x14 78.7 us: shards(): lower_factor = jnp.linalg.cholesky(gram_matrix)]
    all_to_all x0 -> x4, blocking collectives: none -> 75.7 us  [the longest x1 24.1 us: shards(): lax.all_to_all(gram_part.reshape(z_size, slab // z_size * width // lanes,...]
    reduce_scatter x1 -> x0, waiting for transfers between devices: 42.1 us -> none  [shards(): lax.psum_scatter(jnp.concatenate(pieces, axis=1), 'layer', scatter_dimens...]
    pallas_call x0 -> x1, Pallas kernels: none -> 22.6 us  [factor_and_whiten(): pl.pallas_call(functools.partial(factor_kernel, scale), out_shape=(jax.Sh...]
    all_to_all x0 -> x1, waiting for transfers between devices: none -> 11.2 us  [shards(): lax.all_to_all(jnp.broadcast_to(features[None], (group, own_rows, width))...]
    another operation x20 -> x1, local copies, waits for them, and re-layouts: 9.44 us -> 0.76 us
  transfers between devices with their start and end apart: 2 -> 1, of which waited for: 2 -> 1; matrix products, arithmetic and copies ran while one was open for 0% -> 0% of each run, Pallas kernels for 0% -> 0%
where the time goes in v1:
time: 139 us; the launch traced here: 138 us
  blocking collectives  75.7 us (54%)
  Pallas kernels  22.6 us (16%)
  waiting for transfers between devices  11.2 us (8%)
  between operations  10.8 us (8%)
  matrix products  6.6 us (5%)
  local copies, waits for them, and re-layouts  5.46 us (4%)
  starting transfers between devices  4.43 us (3%)
  other arithmetic  1.65 us (1%)
    all_to_all x1, blocking collectives, shards(): lax.all_to_all(gram_part.reshape(z_size, slab // z_size * width // lanes,...  24.1 us
    all_to_all x1, blocking collectives, shards(): lax.all_to_all(jnp.broadcast_to(gram_slab[None], (group,) + gram_slab.sha...  23 us
    pallas_call x1, Pallas kernels, factor_and_whiten(): pl.pallas_call(functools.partial(factor_kernel, scale), out_shape=(jax.Sh...  22.6 us
    all_to_all x1, blocking collectives, shards(): lax.all_to_all(partial.reshape(layers, own_rows, width), 'layer', 0, 0)  14.5 us
    all_to_all x1, blocking collectives, shards(): lax.all_to_all(jnp.broadcast_to(gram_row[None], by_z.shape), 'z', 0, 0)  14.1 us
    all_to_all x1, waiting for transfers between devices, shards(): lax.all_to_all(jnp.broadcast_to(features[None], (group, own_rows, width))...  11.2 us
    dot_general x1, matrix products, shards(): jnp.dot(weighted_rows, grad_rows, preferred_element_type=jnp.float32)  4.61 us
    all_to_all x1, starting transfers between devices, shards(): lax.all_to_all(jnp.broadcast_to(features[None], (group, own_rows, width))...  4.43 us
  transfers between devices with their start and end apart: 1, of which 1 were waited for; matrix products, arithmetic and copies ran while one was open for 0% of the time, Pallas kernels for 0%

profile of v1, /device:TPU:1, one launch (start us, length us, event | category | flops | bytes accessed | tf_op | source)
XLA Modules:
  0.0 138.4 jit_solution(5989429754903030910)
XLA Ops:
  0.6 2.0 %fusion.64 = (s32[1,1]{1,0:T(1,128)}, s32[1,1]{1,0:T(1,128)}, s32[1,1]{1,0:T(1,128)}, s32[1,1]{1,0:T(1,128)}, s32[1,1]{1,0:T(1,128)}, /*index=5*/s32[1,1]{1,0:T(...) fusion(s32[4,4]{1,0:T(4,128)} %bitcast.58), kind=kLoop, calls=%fused_computation.81 | loop fusion | bytes 128 | tf_op jit(solution)/shard_map/slice | solution.py:148
  12.6 0.8 copy.13
  13.3 0.2 reduce-window.8
  13.5 0.1 reduce
  13.6 0.7 sub.11
  14.3 0.7 broadcast_subtract_fusion
  14.9 0.7 convolution_convert_fusion
  15.7 0.0 copy-start.1
  15.7 4.6 %fusion.8 = bf16[512,512]{1,0:T(8,128)(2,1)S(1)} fusion(bf16[1,4096,512]{2,1,0:T(8,128)(2,1)} %param.7, bf16[8,4096]{1,0:T(8,128)(2,1)} %bitcast.60, bf16[64,4096]{1,0:T(8,128)(2,1)S(1)} %convolution_convert_fusion), kind=kOutput, calls=%fused_computation.10 | convolution fusion | flops 2149842944 | bytes 5308416 | tf_op jit(solution)/shard_map/dot_general | solution.py:140
  20.3 0.2 convert_element_type.13
  20.7 0.1 constant_dynamic-slice_fusion.15
  20.8 0.0 copy-done.1
  20.8 0.2 fusion.23
  21.0 0.2 fusion.17
  21.1 0.2 fusion.19
  21.3 0.2 fusion.21
  21.5 14.5 %all_to_all.25 = f32[8,8,512]{2,1,0:T(8,128)S(1)} all-to-all(f32[8,8,512]{2,1,0:T(8,128)S(1)} %maximum_bitcast_fusion), channel_id=1, replica_groups=mesh['layer'=8,'z'=16,'y'=4] {'layer'}, dimensions={0} | all-to-all | bytes 262144 | tf_op jit(solution)/shard_map/all_to_all | solution.py:157
  35.9 0.0 copy-start
  35.9 0.8 broadcast_in_dim.11
  36.8 4.4 %all-to-all-start.1 = ((f32[32,8,512]{2,1,0:T(8,128)}), f32[32,8,512]{2,1,0:T(8,128)S(1)}, u32[]{:S(2)}, u32[]{:S(2)}) async-start(f32[32,8,512]{2,1,0:T(8,128)} %broadcast_in_dim.11), calls=%async_computation.1 | async-start | bytes 1048576 | tf_op jit(solution)/shard_map/all_to_all | solution.py:160
  41.2 11.2 %all-to-all-done.1 = f32[32,8,512]{2,1,0:T(8,128)S(1)} async-done(((f32[32,8,512]{2,1,0:T(8,128)}), f32[32,8,512]{2,1,0:T(8,128)S(1)}, u32[]{:S(2)}, u32[]{:S(2)}) %all-to-all-start.1) | async-done | bytes 524320 | tf_op jit(solution)/shard_map/all_to_all | solution.py:160
  52.4 0.2 copy.15
  52.6 0.6 fusion.15
  53.3 24.1 %all_to_all.26 = f32[16,4,128]{2,1,0:T(4,128)S(1)} all-to-all(f32[16,4,128]{2,1,0:T(4,128)S(1)} %copy.16), channel_id=1, replica_groups=mesh['layer'=8,'z'=16,'y'=4] {'z'}, dimensions={0} | all-to-all | bytes 65536 | tf_op jit(solution)/shard_map/all_to_all | solution.py:170
  77.5 14.1 %all_to_all.27 = f32[16,4,128]{2,1,0:T(4,128)S(1)} all-to-all(f32[16,4,128]{2,1,0:T(4,128)S(1)} %broadcast_in_dim.12), channel_id=1, replica_groups=mesh['layer'=8,'z'=16,'y'=4] {'z'}, dimensions={0} | all-to-all | bytes 65536 | tf_op jit(solution)/shard_map/all_to_all | solution.py:172
  91.5 0.1 broadcast_in_dim.14
  91.6 23.0 %all_to_all.28 = f32[32,64,128]{2,1,0:T(8,128)S(1)} all-to-all(f32[32,64,128]{2,1,0:T(8,128)S(1)} %broadcast_in_dim.14), channel_id=1, replica_groups=mesh['layer'=8,'z'=16,'y'=4] {'layer','y'}, dimensions={0} | all-to-all | bytes 2097152 | tf_op jit(solution)/shard_map/all_to_all | solution.py:174
  114.7 1.1 reshape.102.g_ref
  115.8 0.0 copy-done
  115.8 22.6 %factor_whiten.1 = (f32[8,512]{1,0:T(8,128)}, f32[8,512]{1,0:T(8,128)}) custom-call(s32[1]{0:T(128)} %bitcast.shard_ref, f32[512,512]{1,0:T(8,128)} %reshape.102.g_ref, f32[8,512]{1,0:T(8,128)} %copy-done), custom_call_target="tpu_custom_call" | custom-call | tf_op jit(solution)/shard_map/factor_whiten/pallas_call | solution.py:83
  (5 shorter events, 0.1 us)
Async XLA Ops:
  15.7 5.1 %copy-start.1 = (bf16[1,4,512,128]{3,2,1,0:T(8,128)(2,1)S(1)}, bf16[1,4,512,128]{3,2,1,0:T(8,128)(2,1)}, u32[]{:S(2)}) copy-start(bf16[1,4,512,128]{3,2,1,0:T(8,128)(2,1)} %param.8) | copy-start | bytes 1572868
  35.9 79.9 %copy-start = (f32[8,512]{1,0:T(8,128)}, f32[8,512]{1,0:T(8,128)S(1)}, u32[]{:S(2)}) copy-start(f32[8,512]{1,0:T(8,128)S(1)} %reduce_sum.18.f_ref) | copy-start | bytes 49156
  36.8 15.6 %all-to-all-start.1 = ((f32[32,8,512]{2,1,0:T(8,128)}), f32[32,8,512]{2,1,0:T(8,128)S(1)}, u32[]{:S(2)}, u32[]{:S(2)}) async-start(f32[32,8,512]{2,1,0:T(8,128)} %broadcast_in_dim.11), calls=%async_computation.1 | async-start | bytes 1048576 | tf_op jit(solution)/shard_map/all_to_all | solution.py:160

commit v2 on v1

v2 whole, which is shorter than its diff:
```python
import functools
import math

import jax
import jax.numpy as jnp
from jax import lax
from jax.experimental import pallas as pl
from jax.experimental.pallas import tpu as pltpu
from jax.sharding import Mesh
from jax.sharding import PartitionSpec as P

EX_DEV = 64
HI=lax.Precision.HIGHEST
B=128; S=8; SUB=64
def lane_b(x,l): return jnp.broadcast_to(x[:,l:l+1],x.shape)
def sub_b(x,i): return jnp.broadcast_to(x[i:i+1,:],x.shape)
def dot(a,b,ca,cb):
    return lax.dot_general(a,b,(((ca,),(cb,)),((),())),precision=HI,preferred_element_type=jnp.float32)
def split(x):
    h=x.astype(jnp.bfloat16); r=x-h.astype(jnp.float32)
    m=r.astype(jnp.bfloat16); l=(r-m.astype(jnp.float32)).astype(jnp.bfloat16)
    return h,m,l
def dot_tn(x,y):
    h,m,l=split(x); H,M,L=split(y)
    p=jnp.concatenate([h,h,m,h,m,l],axis=0); q=jnp.concatenate([H,M,H,L,M,H],axis=0)
    return lax.dot_general(p,q,(((0,),(0,)),((),())),preferred_element_type=jnp.float32)
def factor_block(a_ref, off, u_out, i_out, one):
    n=B//S; per=SUB//S
    rows=[a_ref[pl.ds(off+S*g,S),pl.ds(off,B)] for g in range(n)]
    lane=lax.broadcasted_iota(jnp.int32,(S,B),1); sub=lax.broadcasted_iota(jnp.int32,(S,B),0)
    inv=[(lane==sub+S*g).astype(jnp.float32) for g in range(n)]
    for sb in range(0,n,per):
        done_u=[]; done_i=[]
        for s in range(sb,sb+per):
            cols=[[lane_b(rows[g],S*s+k) for k in range(S)] for g in range(s,sb+per)]
            opq=[c*one for c in cols[0]]
            a=[[sub_b(opq[k],i) if i>=k else None for k in range(S)] for i in range(S)]
            low=[[None]*S for _ in range(S)]; d=[None]*S
            ru=[None]*S; ri=[None]*S
            for k in range(S):
                d[k]=lax.rsqrt(a[k][k])
                for i in range(k+1,S): low[i][k]=a[i][k]*d[k]
                for i in range(k+1,S):
                    for j in range(k+1,i+1): a[i][j]=a[i][j]-low[i][k]*low[j][k]
                pu=sub_b(rows[s],k); pi=sub_b(inv[s],k)
                for m in range(k):
                    pu=pu-low[k][m]*ru[m]; pi=pi-low[k][m]*ri[m]
                ru[k]=pu*d[k]; ri[k]=pi*d[k]
            for g in range(s+1,sb+per):
                c=cols[g-s]; lc=[None]*S
                for k in range(S):
                    v=c[k]
                    for m in range(k): v=v-low[k][m]*lc[m]
                    lc[k]=v*d[k]
                for k in range(S):
                    rows[g]=rows[g]-lc[k]*ru[k]; inv[g]=inv[g]-lc[k]*ri[k]
            u=ru[0]; v=ri[0]
            for k in range(1,S):
                u=jnp.where(sub==k,ru[k],u); v=jnp.where(sub==k,ri[k],v)
            u_out[pl.ds(S*s,S),:]=u; i_out[pl.ds(S*s,S),:]=v
            done_u.append(u); done_i.append(v)
        if sb+per<n:
            du=jnp.concatenate(done_u,axis=0); di=jnp.concatenate(done_i,axis=0)
            upd=dot_tn(du,jnp.concatenate([du,di],axis=1))
            for g in range(sb+per,n):
                rows[g]=rows[g]-upd[S*g:S*(g+1),:B]; inv[g]=inv[g]-upd[S*g:S*(g+1),B:]
def factor_kernel(scale,shard_ref,g_ref,f_ref,band_ref,w_ref,a,u,linv,ublk,fs):
    n=a.shape[0]; nb=n//B
    for (kb,q,grp),(owner,unit) in WHERE.items():
        a[kb*B+S*grp:kb*B+S*(grp+1),q*B:(q+1)*B]=g_ref[owner,unit]
    fs[...]=f_ref[...]
    def body(kb,_):
        off=pl.multiple_of(kb*B,B)
        factor_block(a,off,ublk,linv,jnp.where(shard_ref[0]>=0,1.0,0.0))
        r=lax.broadcasted_iota(jnp.int32,(B,B),0); c=lax.broadcasted_iota(jnp.int32,(B,B),1)
        u[pl.ds(off,B),pl.ds(off,B)]=jnp.where(c>=r,ublk[...],0.0)
        for kk in range(nb):
            @pl.when(kb==kk)
            def _():
                lo=kk*B; hi=lo+B
                li=linv[...]
                w=dot(fs[:,lo:hi],li,1,1)
                w_ref[:,lo:hi]=w*scale
                if hi<n:
                    p=dot(li,a[lo:hi,hi:],1,0)
                    u[lo:hi,hi:]=p
                    fs[:,hi:]=fs[:,hi:]-dot(w,p,1,0)
                    for ib in range(kk+1,nb):
                        q=(ib-kk-1)*B
                        a[ib*B:(ib+1)*B,ib*B:]=a[ib*B:(ib+1)*B,ib*B:]-dot(p[:,q:q+B],p[:,q:],0,0)
        return 0
    lax.fori_loop(0,nb,body,0)
    rows=band_ref.shape[0]
    start=pl.multiple_of(shard_ref[0]*rows,rows)
    x=u[pl.ds(start,rows),:]
    r=lax.broadcasted_iota(jnp.int32,x.shape,0)+start; c=lax.broadcasted_iota(jnp.int32,x.shape,1)
    band_ref[...]=jnp.where(c>=r,x,0.0)/scale

def factor_and_whiten(gram, features, shard, scale, side_rows):
    n = features.shape[1]
    return pl.pallas_call(
        functools.partial(factor_kernel, scale),
        out_shape=(
            jax.ShapeDtypeStruct((side_rows, n), jnp.float32),
            jax.ShapeDtypeStruct(features.shape, jnp.float32),
        ),
        in_specs=[
            pl.BlockSpec(memory_space=pltpu.SMEM),
            pl.BlockSpec(memory_space=pltpu.VMEM),
            pl.BlockSpec(memory_space=pltpu.VMEM),
        ],
        out_specs=[pl.BlockSpec(memory_space=pltpu.VMEM)] * 2,
        scratch_shapes=[
            pltpu.VMEM((n, n), jnp.float32),
            pltpu.VMEM((n, n), jnp.float32),
            pltpu.VMEM((B, B), jnp.float32),
            pltpu.VMEM((B, B), jnp.float32),
            pltpu.VMEM(features.shape, jnp.float32),
        ],
        name="factor_whiten",
    )(shard, gram, features)


TILE = 512


def project_kernel(
    index_ref, shard_ref, length_ref, example_ref, adapter_ref, proj_ref, grad_hbm, out_ref,
    grad, left, total, sems,
):
    ranks, slots = adapter_ref.shape
    tiles = slots // TILE

    def fetch(i):
        rows = pl.ds(pl.multiple_of(i * TILE, TILE), TILE)
        return pltpu.make_async_copy(grad_hbm.at[rows, :], grad.at[rows, :], sems.at[i])

    fetch(0).start()
    lengths = length_ref[...].astype(jnp.float32)
    used = jnp.sum(lengths)
    count = lax.div(used.astype(jnp.int32) + (TILE - 1), TILE)

    def begin(i, carry):
        fetch(i).start()
        return carry

    lax.fori_loop(1, count, begin, 0)
    owner = example_ref[...] - shard_ref[0] * EX_DEV
    turns = (EX_DEV, owner.shape[1])
    example = lax.broadcasted_iota(jnp.int32, turns, 0)
    owner = jnp.broadcast_to(owner, turns)
    lengths = jnp.broadcast_to(lengths, turns)
    start = jnp.sum(jnp.where(owner < example, lengths, 0.0), axis=1, keepdims=True)
    end = jnp.sum(jnp.where(owner <= example, lengths, 0.0), axis=1, keepdims=True)
    start = start.astype(jnp.int32)
    end = end.astype(jnp.int32)
    total[...] = jnp.zeros_like(total)

    def step(i, carry):
        first = pl.multiple_of(i * TILE, TILE)
        slot = lax.broadcasted_iota(jnp.int32, (EX_DEV, TILE), 1) + first
        owned = (slot >= start) & (slot < end)
        values = adapter_ref[:, pl.ds(first, TILE)].astype(jnp.float32)
        for r in range(ranks):
            row = jnp.broadcast_to(values[r : r + 1, :], (EX_DEV, TILE))
            left[r * EX_DEV : (r + 1) * EX_DEV, :] = jnp.where(owned, row, 0.0).astype(
                jnp.bfloat16
            )
        fetch(i).wait()
        total[...] += jnp.dot(
            left[...], grad[pl.ds(first, TILE), :], preferred_element_type=jnp.float32
        )
        return carry

    lax.fori_loop(0, count, step, 0)
    per_rank = total.shape[1] // B
    for j in range(proj_ref.shape[0]):
        chosen = []
        for k in range(index_ref.shape[1]):
            block = index_ref[j, k]
            r = lax.div(block, per_rank)
            q = lax.rem(block, per_rank)
            chosen.append(
                total[
                    pl.ds(pl.multiple_of(r * EX_DEV, EX_DEV), EX_DEV),
                    pl.ds(pl.multiple_of(q * B, B), B),
                ].astype(jnp.bfloat16)
            )
        out_ref[:, j * B : (j + 1) * B] = jnp.dot(
            jnp.concatenate(chosen, axis=1), proj_ref[j], preferred_element_type=jnp.float32
        )


def project(index, shard, lengths, examples, adapter, proj, grad):
    slots, width = grad.shape
    ranks = adapter.shape[0]
    smem = pl.BlockSpec(memory_space=pltpu.SMEM)
    vmem = pl.BlockSpec(memory_space=pltpu.VMEM)
    return pl.pallas_call(
        project_kernel,
        out_shape=jax.ShapeDtypeStruct((EX_DEV, proj.shape[0] * proj.shape[2]), jnp.float32),
        in_specs=[smem, smem, vmem, vmem, vmem, vmem, pl.BlockSpec(memory_space=pl.ANY)],
        out_specs=vmem,
        scratch_shapes=[
            pltpu.VMEM((slots, width), grad.dtype),
            pltpu.VMEM((ranks * EX_DEV, TILE), jnp.bfloat16),
            pltpu.VMEM((ranks * EX_DEV, width), jnp.float32),
            pltpu.SemaphoreType.DMA((slots // TILE,)),
        ],
        name="project",
    )(index, shard, lengths[None], examples[None], adapter, proj, grad)


def gram_plan():
    table, where = [], {}
    extra = {t: list(range(10, 16)) for t in range(4)}
    pairs = [(p, q) for p in range(4) for q in range(p + 1, 4)]
    for p, q in pairs:
        for h in range(4):
            side = 0 if h < 2 else 1
            unit = extra[(p, q)[side]].pop(0)
            for i in range(4):
                where[p, q, 4 * h + i] = (len(table), i)
            where[(p, q)[side], (p, q)[side], unit] = (len(table), 4)
            table.append((p, q, h, side, unit))
    for t in range(4):
        for h in range(2):
            for i in range(4):
                where[t, t, 4 * h + i] = (len(table), i)
            where[t, t, 8 + h] = (len(table), 4)
            table.append((t, t, h, 0, 8 + h))
    return table, where


PLAN, WHERE = gram_plan()


def spread_kernel(parts_ref, features_ref, send_ref):
    total = parts_ref[0]
    for i in range(1, parts_ref.shape[0]):
        total = total + parts_ref[i]
    features_ref[...] = total
    for d, (p, q, _, _, _) in enumerate(PLAN):
        send_ref[d, 0] = total[:, p * B : (p + 1) * B]
        send_ref[d, 1] = total[:, q * B : (q + 1) * B]


def spread(parts):
    _, rows, width = parts.shape
    return pl.pallas_call(
        spread_kernel,
        out_shape=(
            jax.ShapeDtypeStruct((rows, width), jnp.float32),
            jax.ShapeDtypeStruct((len(PLAN), 2, rows, B), jnp.float32),
        ),
        in_specs=[pl.BlockSpec(memory_space=pltpu.VMEM)],
        out_specs=[pl.BlockSpec(memory_space=pltpu.VMEM)] * 2,
        name="spread",
    )(parts)


def gram_kernel(role_ref, rows_ref, out_ref, cross, square):
    left = rows_ref[:, 0].reshape(-1, B)
    right = rows_ref[:, 1].reshape(-1, B)
    cross[...] = dot(left, right, 0, 0)
    side = jnp.where(role_ref[1] == 0, left, right)
    square[...] = dot(side, side, 0, 0)
    first = pl.multiple_of(role_ref[0] * 4 * S, 4 * S)
    unit = pl.multiple_of(role_ref[2] * S, S)
    for z in range(out_ref.shape[0]):
        for i in range(4):
            out_ref[z, i] = cross[pl.ds(first + S * i, S), :]
        out_ref[z, 4] = square[pl.ds(unit, S), :]


def gram_units(role, rows, copies):
    return pl.pallas_call(
        gram_kernel,
        out_shape=jax.ShapeDtypeStruct((copies, 5, S, B), jnp.float32),
        in_specs=[pl.BlockSpec(memory_space=pltpu.SMEM), pl.BlockSpec(memory_space=pltpu.VMEM)],
        out_specs=pl.BlockSpec(memory_space=pltpu.VMEM),
        scratch_shapes=[pltpu.VMEM((B, B), jnp.float32), pltpu.VMEM((B, B), jnp.float32)],
        name="gram_units",
    )(role, rows)


def shards(
    adapter_input,
    output_gradient,
    projection,
    input_block_index,
    turn_token_length,
    turn_to_example,
):
    adapter_rows = adapter_input[0]
    grad_rows = output_gradient[0]
    proj_blocks = projection[0]
    picked = input_block_index[0]
    layers = lax.axis_size("layer")
    far_size = lax.axis_size("zh")
    near_size = lax.axis_size("zl")
    y_size = lax.axis_size("y")
    shard_count = far_size * near_size * y_size
    shard = lax.axis_index(("zh", "zl", "y"))
    shard = shard.astype(jnp.int32)[None]
    partial = project(
        picked, shard, turn_token_length, turn_to_example, adapter_rows, proj_blocks, grad_rows
    )
    width = partial.shape[1]
    own_rows = EX_DEV // layers
    by_layer = lax.all_to_all(partial.reshape(layers, own_rows, width), "layer", 0, 0)
    features, outgoing = spread(by_layer)
    group = layers * y_size
    plane = lax.all_to_all(outgoing, ("layer", "y"), 0, 0)
    mine = lax.axis_index("layer") * y_size + lax.axis_index("y")
    role = lax.dynamic_index_in_dim(
        jnp.array([entry[2:] for entry in PLAN], jnp.int32), mine, 0, keepdims=False
    )
    packed = gram_units(role, plane, near_size)
    by_near = lax.all_to_all(packed, "zl", 0, 0)
    nearby = jnp.sum(by_near, axis=0)
    by_far = lax.all_to_all(jnp.broadcast_to(nearby[None], (far_size,) + nearby.shape), "zh", 0, 0)
    summed = jnp.sum(by_far, axis=0)
    gram_tiles = lax.all_to_all(
        jnp.broadcast_to(summed[None], (group,) + summed.shape), ("layer", "y"), 0, 0
    )
    scale = math.sqrt(EX_DEV * shard_count)
    band, whitened = factor_and_whiten(
        gram_tiles, features, shard, scale, width // shard_count
    )
    return (band, whitened)


def solution(mesh):
    layer_count, shard_count = mesh.devices.shape
    y_size = 4
    near_size = 4
    fine = Mesh(
        mesh.devices.reshape(
            layer_count, shard_count // (near_size * y_size), near_size, y_size
        ),
        ("layer", "zh", "zl", "y"),
    )
    part = ("zh", "zl", "y")
    in_specs = (
        P("layer", None, part),
        P("layer", part, None),
        P("layer", None, None, None),
        P("layer", None, None),
        P(part),
        P(part),
    )
    out_specs = (P(part, None), P(part + ("layer",), None))
    return jax.shard_map(shards, mesh=fine, in_specs=in_specs, out_specs=out_specs, check_vma=False)
```

time: 139 us -> 106 us (0.76)
  between operations: 10.8 us -> 0.69 us
  blocking collectives: 75.7 us -> 66.7 us
  matrix products: 6.6 us -> 0 us
  waiting for transfers between devices: 11.2 us -> 7.67 us
  local copies, waits for them, and re-layouts: 5.46 us -> 1.95 us
  other arithmetic: 1.65 us -> 0.02 us
    all_to_all x3, blocking collectives: 61.2 us -> 50.6 us  [the longest x1 23.6 us: shards(): lax.all_to_all(jnp.broadcast_to(nearby[None], (far_size,) + nearby.shape)...]
    pallas_call x0 -> x3, Pallas kernels: none -> 7.66 us  [the longest x1 4.03 us: project(): pl.pallas_call(project_kernel, out_shape=jax.ShapeDtypeStruct((EX_DEV, pr...]
    dot_general x7 -> x0, matrix products: 6.6 us -> none  [the longest x1 4.61 us: shards(): jnp.dot(weighted_rows, grad_rows, preferred_element_type=jnp.float32)]
    pallas_call x1, Pallas kernels: 22.6 us -> 16 us  [factor_and_whiten(): pl.pallas_call(functools.partial(factor_kernel, scale), out_shape=(jax.Sh...]
    all_to_all x1, waiting for transfers between devices: 11.2 us -> 7.67 us  [shards(): plane = lax.all_to_all(outgoing, ('layer', 'y'), 0, 0)]
    slice x1 -> x0, local copies, waits for them, and re-layouts: 1.97 us -> none  [shards(): picked[column, slot_index] * 128]
    all_to_all x1, blocking collectives: 14.5 us -> 16.1 us  [shards(): lax.all_to_all(partial.reshape(layers, own_rows, width), 'layer', 0, 0)]
  transfers between devices with their start and end apart: 1 -> 1, of which waited for: 1 -> 1; matrix products, arithmetic and copies ran while one was open for 0% -> 1% of each run, Pallas kernels for 0% -> 0%
where the time goes in v2:
time: 106 us; the launch traced here: 105 us
  blocking collectives  66.7 us (63%)
  Pallas kernels  23.7 us (22%)
  waiting for transfers between devices  7.67 us (7%)
  starting transfers between devices  4.4 us (4%)
  local copies, waits for them, and re-layouts  1.95 us (2%)
    all_to_all x1, blocking collectives, shards(): lax.all_to_all(jnp.broadcast_to(nearby[None], (far_size,) + nearby.shape)...  23.6 us
    all_to_all x1, blocking collectives, shards(): lax.all_to_all(jnp.broadcast_to(summed[None], (group,) + summed.shape), (...  19.1 us
    all_to_all x1, blocking collectives, shards(): lax.all_to_all(partial.reshape(layers, own_rows, width), 'layer', 0, 0)  16.1 us
    pallas_call x1, Pallas kernels, factor_and_whiten(): pl.pallas_call(functools.partial(factor_kernel, scale), out_shape=(jax.Sh...  16 us
    all_to_all x1, blocking collectives, shards(): by_near = lax.all_to_all(packed, 'zl', 0, 0)  7.91 us
    all_to_all x1, waiting for transfers between devices, shards(): plane = lax.all_to_all(outgoing, ('layer', 'y'), 0, 0)  7.67 us
    all_to_all x1, starting transfers between devices, shards(): plane = lax.all_to_all(outgoing, ('layer', 'y'), 0, 0)  4.4 us
    pallas_call x1, Pallas kernels, project(): pl.pallas_call(project_kernel, out_shape=jax.ShapeDtypeStruct((EX_DEV, pr...  4.03 us
  transfers between devices with their start and end apart: 1, of which 1 were waited for; matrix products, arithmetic and copies ran while one was open for 1% of the time, Pallas kernels for 0%

profile of v2, /device:TPU:1, one launch (start us, length us, event | category | flops | bytes accessed | tf_op | source)
XLA Modules:
  0.0 105.1 jit_solution(16310086198795185673)
XLA Ops:
  0.6 4.0 %project.1 = f32[64,512]{1,0:T(8,128)} custom-call(s32[4,4]{1,0:T(4,128)} %bitcast.14, s32[1]{0:T(128)} %bitcast.shard_ref, s32[1,128]{1,0:T(1,128)} %bitcast.15, s32[1,128]{1,0:T(1,128)} %bitcast.16, bf16[8,4096]{1,0:T(8,128)(2,1)} %bitcast.13, bf16[4,512,128]{2,1,0:T(8,128)(2,1)} %bitcast.11, bf16[4096,512]{1,0:T(8,128)(2,1)} %bitcast.10), custom_call_target="tpu_custom_call" | custom-call | tf_op jit(solution)/shard_map/project/pallas_call | solution.py:199
  4.7 16.1 %all_to_all.25.parts_ref = f32[8,8,512]{2,1,0:T(8,128)} all-to-all(f32[8,8,512]{2,1,0:T(8,128)} %bitcast.12), channel_id=1, replica_groups=mesh['layer'=8,'zh'=4,'zl'=4,'y'=4] {'layer'}, dimensions={0} | all-to-all | bytes 262144 | tf_op jit(solution)/shard_map/all_to_all | solution.py:311
  20.7 1.6 %spread.1 = (f32[8,512]{1,0:T(8,128)}, f32[32,2,8,128]{3,2,1,0:T(8,128)}) custom-call(f32[8,8,512]{2,1,0:T(8,128)} %all_to_all.25.parts_ref), custom_call_target="tpu_custom_call" | custom-call | tf_op jit(solution)/shard_map/spread/pallas_call | solution.py:250
  22.4 4.4 %all-to-all-start.1 = ((f32[32,2,8,128]{3,2,1,0:T(8,128)}), f32[32,2,8,128]{3,2,1,0:T(8,128)S(1)}, u32[]{:S(2)}, u32[]{:S(2)}) async-start(f32[32,2,8,128]{3,2,1,0:T(8,128)} %get-tuple-element.4), calls=%async_computation.1 | async-start | bytes 524288 | tf_op jit(solution)/shard_map/all_to_all | solution.py:314
  26.8 1.2 %dynamic-slice_bitcast_fusion.role_ref = s32[3]{0:T(128)} fusion(s32[32,3]{1,0:T(8,128)} %constant.31.clone, s32[]{:T(128)S(6)} %select_n.4), kind=kLoop, calls=%fused_computation | loop fusion | bytes 28 | tf_op jit(solution)/shard_map/jit(dynamic_index_in_dim)/squeeze | solution.py:316
  28.0 7.7 %all-to-all-done.1.rows_ref = f32[32,2,8,128]{3,2,1,0:T(8,128)S(1)} async-done(((f32[32,2,8,128]{3,2,1,0:T(8,128)}), f32[32,2,8,128]{3,2,1,0:T(8,128)S(1)}, u32[]{:S(2)}, u32[]{:S(2)}) %all-to-all-start.1) | async-done | bytes 262176 | tf_op jit(solution)/shard_map/all_to_all | solution.py:314
  35.7 0.0 copy-start
  35.7 0.7 copy-done
  36.4 2.0 %gram_units.1 = f32[4,5,8,128]{3,2,1,0:T(8,128)} custom-call(s32[3]{0:T(128)} %dynamic-slice_bitcast_fusion.role_ref, f32[32,2,8,128]{3,2,1,0:T(8,128)} %copy-done), custom_call_target="tpu_custom_call" | custom-call | tf_op jit(solution)/shard_map/gram_units/pallas_call | solution.py:277
  38.4 7.9 %all_to_all.26 = f32[4,5,8,128]{3,2,1,0:T(8,128)S(1)} all-to-all(f32[4,5,8,128]{3,2,1,0:T(8,128)} %gram_units.1), channel_id=1, replica_groups=mesh['layer'=8,'zh'=4,'zl'=4,'y'=4] {'zl'}, dimensions={0} | all-to-all | bytes 163840 | tf_op jit(solution)/shard_map/all_to_all | solution.py:320
  46.3 23.6 %all_to_all.27 = f32[4,5,8,128]{3,2,1,0:T(8,128)S(1)} all-to-all(f32[4,5,8,128]{3,2,1,0:T(8,128)S(1)} %broadcast_in_dim.24), channel_id=1, replica_groups=mesh['layer'=8,'zh'=4,'zl'=4,'y'=4] {'zh'}, dimensions={0} | all-to-all | bytes 163840 | tf_op jit(solution)/shard_map/all_to_all | solution.py:322
  69.9 19.1 %all_to_all.28.g_ref = f32[32,5,8,128]{3,2,1,0:T(8,128)} all-to-all(f32[32,5,8,128]{3,2,1,0:T(8,128)S(1)} %broadcast_in_dim.25), channel_id=1, replica_groups=mesh['layer'=8,'zh'=4,'zl'=4,'y'=4] {'layer','y'}, dimensions={0} | all-to-all | bytes 1310720 | tf_op jit(solution)/shard_map/all_to_all | solution.py:324
  89.0 16.0 %factor_whiten.1 = (f32[8,512]{1,0:T(8,128)}, f32[8,512]{1,0:T(8,128)}) custom-call(s32[1]{0:T(128)} %bitcast.shard_ref, f32[32,5,8,128]{3,2,1,0:T(8,128)} %all_to_all.28.g_ref, f32[8,512]{1,0:T(8,128)} %get-tuple-element.5.f_ref), custom_call_target="tpu_custom_call" | custom-call | tf_op jit(solution)/shard_map/factor_whiten/pallas_call | solution.py:101
  (4 shorter events, 0.1 us)
Async XLA Ops:
  22.4 13.3 %all-to-all-start.1 = ((f32[32,2,8,128]{3,2,1,0:T(8,128)}), f32[32,2,8,128]{3,2,1,0:T(8,128)S(1)}, u32[]{:S(2)}, u32[]{:S(2)}) async-start(f32[32,2,8,128]{3,2,1,0:T(8,128)} %get-tuple-element.4), calls=%async_computation.1 | async-start | bytes 524288 | tf_op jit(solution)/shard_map/all_to_all | solution.py:314
  35.7 0.7 copy-start

commit v3 on v2

--- a/solution.py
+++ b/solution.py
@@ -117,6 +117,7 @@
             pltpu.VMEM((B, B), jnp.float32),
             pltpu.VMEM(features.shape, jnp.float32),
         ],
+        compiler_params=pltpu.CompilerParams(vmem_limit_bytes=12 << 20),
         name="factor_whiten",
     )(shard, gram, features)
 
@@ -125,17 +126,26 @@
 
 
 def project_kernel(
-    index_ref, shard_ref, length_ref, example_ref, adapter_ref, proj_ref, grad_hbm, out_ref,
-    grad, left, total, sems,
+    index_hbm, length_hbm, example_hbm, adapter_hbm, proj_hbm, grad_hbm, out_ref,
+    index_ref, length_ref, example_ref, adapter_ref, proj_ref, grad, left, total, sems, arrivals,
 ):
     ranks, slots = adapter_ref.shape
-    tiles = slots // TILE
 
     def fetch(i):
         rows = pl.ds(pl.multiple_of(i * TILE, TILE), TILE)
         return pltpu.make_async_copy(grad_hbm.at[rows, :], grad.at[rows, :], sems.at[i])
 
+    lengths_in = pltpu.make_async_copy(length_hbm, length_ref, arrivals.at[0])
+    examples_in = pltpu.make_async_copy(example_hbm, example_ref, arrivals.at[1])
+    adapter_in = pltpu.make_async_copy(adapter_hbm, adapter_ref, arrivals.at[2])
+    index_in = pltpu.make_async_copy(index_hbm, index_ref, arrivals.at[3])
+    proj_in = pltpu.make_async_copy(proj_hbm, proj_ref, arrivals.at[4])
+    lengths_in.start()
+    examples_in.start()
     fetch(0).start()
+    adapter_in.start()
+    index_in.start()
+    lengths_in.wait()
     lengths = length_ref[...].astype(jnp.float32)
     used = jnp.sum(lengths)
     count = lax.div(used.astype(jnp.int32) + (TILE - 1), TILE)
@@ -145,7 +155,9 @@
         return carry
 
     lax.fori_loop(1, count, begin, 0)
-    owner = example_ref[...] - shard_ref[0] * EX_DEV
+    proj_in.start()
+    examples_in.wait()
+    owner = example_ref[...] - example_ref[:, :1]
     turns = (EX_DEV, owner.shape[1])
     example = lax.broadcasted_iota(jnp.int32, turns, 0)
     owner = jnp.broadcast_to(owner, turns)
@@ -155,6 +167,7 @@
     start = start.astype(jnp.int32)
     end = end.astype(jnp.int32)
     total[...] = jnp.zeros_like(total)
+    adapter_in.wait()
 
     def step(i, carry):
         first = pl.multiple_of(i * TILE, TILE)
@@ -173,6 +186,8 @@
         return carry
 
     lax.fori_loop(0, count, step, 0)
+    index_in.wait()
+    proj_in.wait()
     per_rank = total.shape[1] // B
     for j in range(proj_ref.shape[0]):
         chosen = []
@@ -191,24 +206,29 @@
         )
 
 
-def project(index, shard, lengths, examples, adapter, proj, grad):
+def project(index, lengths, examples, adapter, proj, grad):
     slots, width = grad.shape
     ranks = adapter.shape[0]
-    smem = pl.BlockSpec(memory_space=pltpu.SMEM)
-    vmem = pl.BlockSpec(memory_space=pltpu.VMEM)
     return pl.pallas_call(
         project_kernel,
         out_shape=jax.ShapeDtypeStruct((EX_DEV, proj.shape[0] * proj.shape[2]), jnp.float32),
-        in_specs=[smem, smem, vmem, vmem, vmem, vmem, pl.BlockSpec(memory_space=pl.ANY)],
-        out_specs=vmem,
+        in_specs=[pl.BlockSpec(memory_space=pltpu.HBM)] * 6,
+        out_specs=pl.BlockSpec(memory_space=pltpu.VMEM),
         scratch_shapes=[
+            pltpu.SMEM(index.shape, index.dtype),
+            pltpu.VMEM((1,) + lengths.shape, lengths.dtype),
+            pltpu.VMEM((1,) + examples.shape, examples.dtype),
+            pltpu.VMEM(adapter.shape, adapter.dtype),
+            pltpu.VMEM(proj.shape, proj.dtype),
             pltpu.VMEM((slots, width), grad.dtype),
             pltpu.VMEM((ranks * EX_DEV, TILE), jnp.bfloat16),
             pltpu.VMEM((ranks * EX_DEV, width), jnp.float32),
             pltpu.SemaphoreType.DMA((slots // TILE,)),
+            pltpu.SemaphoreType.DMA((5,)),
         ],
+        compiler_params=pltpu.CompilerParams(vmem_limit_bytes=59 << 20),
         name="project",
-    )(index, shard, lengths[None], examples[None], adapter, proj, grad)
+    )(index, lengths[None], examples[None], adapter, proj, grad)
 
 
 def gram_plan():
@@ -255,33 +275,36 @@
         ),
         in_specs=[pl.BlockSpec(memory_space=pltpu.VMEM)],
         out_specs=[pl.BlockSpec(memory_space=pltpu.VMEM)] * 2,
+        compiler_params=pltpu.CompilerParams(vmem_limit_bytes=4 << 20),
         name="spread",
     )(parts)
 
 
-def gram_kernel(role_ref, rows_ref, out_ref, cross, square):
+def gram_kernel(mine_ref, table_ref, rows_ref, out_ref, cross, square):
+    mine = mine_ref[0]
     left = rows_ref[:, 0].reshape(-1, B)
     right = rows_ref[:, 1].reshape(-1, B)
     cross[...] = dot(left, right, 0, 0)
-    side = jnp.where(role_ref[1] == 0, left, right)
+    side = jnp.where(table_ref[mine, 1] == 0, left, right)
     square[...] = dot(side, side, 0, 0)
-    first = pl.multiple_of(role_ref[0] * 4 * S, 4 * S)
-    unit = pl.multiple_of(role_ref[2] * S, S)
+    first = pl.multiple_of(table_ref[mine, 0] * 4 * S, 4 * S)
+    unit = pl.multiple_of(table_ref[mine, 2] * S, S)
     for z in range(out_ref.shape[0]):
         for i in range(4):
             out_ref[z, i] = cross[pl.ds(first + S * i, S), :]
         out_ref[z, 4] = square[pl.ds(unit, S), :]
 
 
-def gram_units(role, rows, copies):
+def gram_units(mine, rows, copies):
     return pl.pallas_call(
         gram_kernel,
         out_shape=jax.ShapeDtypeStruct((copies, 5, S, B), jnp.float32),
-        in_specs=[pl.BlockSpec(memory_space=pltpu.SMEM), pl.BlockSpec(memory_space=pltpu.VMEM)],
+        in_specs=[pl.BlockSpec(memory_space=pltpu.SMEM)] * 2 + [pl.BlockSpec(memory_space=pltpu.VMEM)],
         out_specs=pl.BlockSpec(memory_space=pltpu.VMEM),
         scratch_shapes=[pltpu.VMEM((B, B), jnp.float32), pltpu.VMEM((B, B), jnp.float32)],
+        compiler_params=pltpu.CompilerParams(vmem_limit_bytes=4 << 20),
         name="gram_units",
-    )(role, rows)
+    )(mine, jnp.array([entry[2:] for entry in PLAN], jnp.int32), rows)
 
 
 def shards(
@@ -304,19 +327,17 @@
     shard = lax.axis_index(("zh", "zl", "y"))
     shard = shard.astype(jnp.int32)[None]
     partial = project(
-        picked, shard, turn_token_length, turn_to_example, adapter_rows, proj_blocks, grad_rows
-    )
+        picked, turn_token_length, turn_to_example, adapter_rows, proj_blocks, grad_rows
+    )
+    mine = (lax.axis_index("layer") * y_size + lax.axis_index("y")).astype(jnp.int32)[None]
+    partial, mine, shard = lax.optimization_barrier((partial, mine, shard))
     width = partial.shape[1]
     own_rows = EX_DEV // layers
     by_layer = lax.all_to_all(partial.reshape(layers, own_rows, width), "layer", 0, 0)
     features, outgoing = spread(by_layer)
     group = layers * y_size
     plane = lax.all_to_all(outgoing, ("layer", "y"), 0, 0)
-    mine = lax.axis_index("layer") * y_size + lax.axis_index("y")
-    role = lax.dynamic_index_in_dim(
-        jnp.array([entry[2:] for entry in PLAN], jnp.int32), mine, 0, keepdims=False
-    )
-    packed = gram_units(role, plane, near_size)
+    packed = gram_units(mine, plane, near_size)
     by_near = lax.all_to_all(packed, "zl", 0, 0)
     nearby = jnp.sum(by_near, axis=0)
     by_far = lax.all_to_all(jnp.broadcast_to(nearby[None], (far_size,) + nearby.shape), "zh", 0, 0)

time: 106 us -> 99.5 us (0.939)
  blocking collectives: 66.7 us -> 78.3 us
  waiting for transfers between devices: 7.67 us -> 0 us
  starting transfers between devices: 4.4 us -> 0 us
  Pallas kernels: 23.7 us -> 20.4 us
  local copies, waits for them, and re-layouts: 1.95 us -> 0.06 us
    all_to_all x0 -> x1, blocking collectives: none -> 12.4 us  [shards(): plane = lax.all_to_all(outgoing, ('layer', 'y'), 0, 0)]
    all_to_all x1 -> x0, waiting for transfers between devices: 7.67 us -> none  [shards(): plane = lax.all_to_all(outgoing, ('layer', 'y'), 0, 0)]
    all_to_all x1 -> x0, starting transfers between devices: 4.4 us -> none  [shards(): plane = lax.all_to_all(outgoing, ('layer', 'y'), 0, 0)]
    pallas_call x1, Pallas kernels: 1.63 us -> 0.03 us  [spread(): pl.pallas_call(spread_kernel, out_shape=(jax.ShapeDtypeStruct((rows, widt...]
    squeeze x1 -> x0, local copies, waits for them, and re-layouts: 1.21 us -> none  [shards(): lax.dynamic_index_in_dim(jnp.array([entry[2:] for entry in PLAN], jnp.int...]
    pallas_call x1, Pallas kernels: 16 us -> 14.9 us  [factor_and_whiten(): pl.pallas_call(functools.partial(factor_kernel, scale), out_shape=(jax.Sh...]
  transfers between devices with their start and end apart: 1 -> 0, of which waited for: 1 -> 0; matrix products, arithmetic and copies ran while one was open for 1% -> 0% of each run, Pallas kernels for 0% -> 0%
where the time goes in v3:
time: 99.5 us
  blocking collectives  78.3 us (79%)
  Pallas kernels  20.4 us (21%)
    all_to_all x1, blocking collectives, shards(): lax.all_to_all(jnp.broadcast_to(nearby[None], (far_size,) + nearby.shape)...  23.8 us
    all_to_all x1, blocking collectives, shards(): lax.all_to_all(jnp.broadcast_to(summed[None], (group,) + summed.shape), (...  18.9 us
    all_to_all x1, blocking collectives, shards(): lax.all_to_all(partial.reshape(layers, own_rows, width), 'layer', 0, 0)  15.4 us
    pallas_call x1, Pallas kernels, factor_and_whiten(): pl.pallas_call(functools.partial(factor_kernel, scale), out_shape=(jax.Sh...  14.9 us
    all_to_all x1, blocking collectives, shards(): plane = lax.all_to_all(outgoing, ('layer', 'y'), 0, 0)  12.4 us
    all_to_all x1, blocking collectives, shards(): by_near = lax.all_to_all(packed, 'zl', 0, 0)  7.82 us
    pallas_call x1, Pallas kernels, project(): pl.pallas_call(project_kernel, out_shape=jax.ShapeDtypeStruct((EX_DEV, pr...  4.24 us

profile of v3, /device:TPU:1, one launch (start us, length us, event | category | flops | bytes accessed | tf_op | source)
XLA Modules:
  0.0 99.5 jit_solution(3744729949854393695)
XLA Ops:
  0.6 0.0 copy-start
  0.7 4.2 %project.1 = f32[64,512]{1,0:T(8,128)} custom-call(s32[4,4]{1,0:T(4,128)} %bitcast.13, s32[1,128]{1,0:T(1,128)} %bitcast.14, s32[1,128]{1,0:T(1,128)} %bitcast.15, bf16[8,4096]{1,0:T(8,128)(2,1)} %bitcast.12, bf16[4,512,128]{2,1,0:T(8,128)(2,1)} %bitcast.10, bf16[4096,512]{1,0:T(8,128)(2,1)} %bitcast.9), custom_call_target="tpu_custom_call" | custom-call | tf_op jit(solution)/shard_map/project/pallas_call | solution.py:212
  4.9 15.4 %all_to_all.25.parts_ref = f32[8,8,512]{2,1,0:T(8,128)S(1)} all-to-all(f32[8,8,512]{2,1,0:T(8,128)} %bitcast.11), channel_id=1, replica_groups=mesh['layer'=8,'zh'=4,'zl'=4,'y'=4] {'layer'}, dimensions={0} | all-to-all | bytes 262144 | tf_op jit(solution)/shard_map/all_to_all | solution.py:336
  20.3 12.4 %all_to_all.26.rows_ref = f32[32,2,8,128]{3,2,1,0:T(8,128)S(1)} all-to-all(f32[32,2,8,128]{3,2,1,0:T(8,128)S(1)} %get-tuple-element.10), channel_id=1, replica_groups=mesh['layer'=8,'zh'=4,'zl'=4,'y'=4] {'layer','y'}, dimensions={0} | all-to-all | bytes 524288 | tf_op jit(solution)/shard_map/all_to_all | solution.py:339
  32.7 0.0 copy-done
  32.7 1.2 %gram_units.1 = f32[4,5,8,128]{3,2,1,0:T(8,128)S(1)} custom-call(s32[1]{0:T(128)} %bitcast.6.mine_ref, s32[32,3]{1,0:T(8,128)S(1)} %copy-done, f32[32,2,8,128]{3,2,1,0:T(8,128)S(1)} %all_to_all.26.rows_ref), custom_call_target="tpu_custom_call" | custom-call | tf_op jit(solution)/shard_map/gram_units/pallas_call | solution.py:299
  33.9 7.8 %all_to_all.27 = f32[4,5,8,128]{3,2,1,0:T(8,128)S(1)} all-to-all(f32[4,5,8,128]{3,2,1,0:T(8,128)S(1)} %gram_units.1), channel_id=1, replica_groups=mesh['layer'=8,'zh'=4,'zl'=4,'y'=4] {'zl'}, dimensions={0} | all-to-all | bytes 163840 | tf_op jit(solution)/shard_map/all_to_all | solution.py:341
  41.8 23.8 %all_to_all.28 = f32[4,5,8,128]{3,2,1,0:T(8,128)S(1)} all-to-all(f32[4,5,8,128]{3,2,1,0:T(8,128)S(1)} %broadcast_in_dim.28), channel_id=1, replica_groups=mesh['layer'=8,'zh'=4,'zl'=4,'y'=4] {'zh'}, dimensions={0} | all-to-all | bytes 163840 | tf_op jit(solution)/shard_map/all_to_all | solution.py:343
  65.6 18.9 %all_to_all.29.g_ref = f32[32,5,8,128]{3,2,1,0:T(8,128)S(1)} all-to-all(f32[32,5,8,128]{3,2,1,0:T(8,128)S(1)} %broadcast_in_dim.29), channel_id=1, replica_groups=mesh['layer'=8,'zh'=4,'zl'=4,'y'=4] {'layer','y'}, dimensions={0} | all-to-all | bytes 1310720 | tf_op jit(solution)/shard_map/all_to_all | solution.py:345
  84.5 14.9 %factor_whiten.1 = (f32[8,512]{1,0:T(8,128)}, f32[8,512]{1,0:T(8,128)}) custom-call(s32[1]{0:T(128)} %bitcast.7.shard_ref, f32[32,5,8,128]{3,2,1,0:T(8,128)S(1)} %all_to_all.29.g_ref, f32[8,512]{1,0:T(8,128)S(1)} %get-tuple-element.11.f_ref), custom_call_target="tpu_custom_call" | custom-call | tf_op jit(solution)/shard_map/factor_whiten/pallas_call | solution.py:101
  (5 shorter events, 0.1 us)
Async XLA Ops:
  0.6 32.1 %copy-start = (s32[32,3]{1,0:T(8,128)S(1)}, s32[32,3]{1,0:T(8,128)}, u32[]{:S(2)}) copy-start(s32[32,3]{1,0:T(8,128)} %constant.25.clone.table_ref) | copy-start | bytes 1156

commit v4 on v3

--- a/solution.py
+++ b/solution.py
@@ -16,6 +16,11 @@
 def sub_b(x,i): return jnp.broadcast_to(x[i:i+1,:],x.shape)
 def dot(a,b,ca,cb):
     return lax.dot_general(a,b,(((ca,),(cb,)),((),())),precision=HI,preferred_element_type=jnp.float32)
+def dot3(a,b,ca,cb):
+    h=a.astype(jnp.bfloat16); l=(a-h.astype(jnp.float32)).astype(jnp.bfloat16)
+    H=b.astype(jnp.bfloat16); L=(b-H.astype(jnp.float32)).astype(jnp.bfloat16)
+    f=lambda x,y: lax.dot_general(x,y,(((ca,),(cb,)),((),())),preferred_element_type=jnp.float32)
+    return f(h,H)+(f(h,L)+f(l,H))
 def split(x):
     h=x.astype(jnp.bfloat16); r=x-h.astype(jnp.float32)
     m=r.astype(jnp.bfloat16); l=(r-m.astype(jnp.float32)).astype(jnp.bfloat16)
@@ -79,15 +84,15 @@
             def _():
                 lo=kk*B; hi=lo+B
                 li=linv[...]
-                w=dot(fs[:,lo:hi],li,1,1)
+                w=dot3(fs[:,lo:hi],li,1,1)
                 w_ref[:,lo:hi]=w*scale
                 if hi<n:
-                    p=dot(li,a[lo:hi,hi:],1,0)
+                    p=dot3(li,a[lo:hi,hi:],1,0)
                     u[lo:hi,hi:]=p
-                    fs[:,hi:]=fs[:,hi:]-dot(w,p,1,0)
+                    fs[:,hi:]=fs[:,hi:]-dot3(w,p,1,0)
                     for ib in range(kk+1,nb):
                         q=(ib-kk-1)*B
-                        a[ib*B:(ib+1)*B,ib*B:]=a[ib*B:(ib+1)*B,ib*B:]-dot(p[:,q:q+B],p[:,q:],0,0)
+                        a[ib*B:(ib+1)*B,ib*B:]=a[ib*B:(ib+1)*B,ib*B:]-dot3(p[:,q:q+B],p[:,q:],0,0)
         return 0
     lax.fori_loop(0,nb,body,0)
     rows=band_ref.shape[0]

time: 99.5 us -> 99.1 us (level)
  Pallas kernels: 20.4 us -> 18.9 us
    all_to_all x1, blocking collectives: 7.82 us -> 9.22 us  [shards(): by_near = lax.all_to_all(packed, 'zl', 0, 0)]
where the time goes in v4:
time: 99.1 us; the launch traced here: 98.6 us
  blocking collectives  78.9 us (80%)
  Pallas kernels  18.9 us (19%)
    all_to_all x1, blocking collectives, shards(): lax.all_to_all(jnp.broadcast_to(nearby[None], (far_size,) + nearby.shape)...  23 us
    all_to_all x1, blocking collectives, shards(): lax.all_to_all(jnp.broadcast_to(summed[None], (group,) + summed.shape), (...  18.9 us
    all_to_all x1, blocking collectives, shards(): lax.all_to_all(partial.reshape(layers, own_rows, width), 'layer', 0, 0)  15.4 us
    pallas_call x1, Pallas kernels, factor_and_whiten(): pl.pallas_call(functools.partial(factor_kernel, scale), out_shape=(jax.Sh...  14.4 us
    all_to_all x1, blocking collectives, shards(): plane = lax.all_to_all(outgoing, ('layer', 'y'), 0, 0)  12.4 us
    all_to_all x1, blocking collectives, shards(): by_near = lax.all_to_all(packed, 'zl', 0, 0)  9.22 us
    pallas_call x1, Pallas kernels, project(): pl.pallas_call(project_kernel, out_shape=jax.ShapeDtypeStruct((EX_DEV, pr...  3.32 us

profile of v4, /device:TPU:1, one launch (start us, length us, event | category | flops | bytes accessed | tf_op | source)
XLA Modules:
  0.0 98.6 jit_solution(4664918540839126770)
XLA Ops:
  0.6 0.0 copy-start
  0.7 3.3 %project.1 = f32[64,512]{1,0:T(8,128)} custom-call(s32[4,4]{1,0:T(4,128)} %bitcast.13, s32[1,128]{1,0:T(1,128)} %bitcast.14, s32[1,128]{1,0:T(1,128)} %bitcast.15, bf16[8,4096]{1,0:T(8,128)(2,1)} %bitcast.12, bf16[4,512,128]{2,1,0:T(8,128)(2,1)} %bitcast.10, bf16[4096,512]{1,0:T(8,128)(2,1)} %bitcast.9), custom_call_target="tpu_custom_call" | custom-call | tf_op jit(solution)/shard_map/project/pallas_call | solution.py:217
  4.0 15.4 %all_to_all.25.parts_ref = f32[8,8,512]{2,1,0:T(8,128)S(1)} all-to-all(f32[8,8,512]{2,1,0:T(8,128)} %bitcast.11), channel_id=1, replica_groups=mesh['layer'=8,'zh'=4,'zl'=4,'y'=4] {'layer'}, dimensions={0} | all-to-all | bytes 262144 | tf_op jit(solution)/shard_map/all_to_all | solution.py:341
  19.4 12.4 %all_to_all.26.rows_ref = f32[32,2,8,128]{3,2,1,0:T(8,128)S(1)} all-to-all(f32[32,2,8,128]{3,2,1,0:T(8,128)S(1)} %get-tuple-element.10), channel_id=1, replica_groups=mesh['layer'=8,'zh'=4,'zl'=4,'y'=4] {'layer','y'}, dimensions={0} | all-to-all | bytes 524288 | tf_op jit(solution)/shard_map/all_to_all | solution.py:344
  31.8 0.0 copy-done
  31.8 1.2 %gram_units.1 = f32[4,5,8,128]{3,2,1,0:T(8,128)S(1)} custom-call(s32[1]{0:T(128)} %bitcast.6.mine_ref, s32[32,3]{1,0:T(8,128)S(1)} %copy-done, f32[32,2,8,128]{3,2,1,0:T(8,128)S(1)} %all_to_all.26.rows_ref), custom_call_target="tpu_custom_call" | custom-call | tf_op jit(solution)/shard_map/gram_units/pallas_call | solution.py:304
  33.0 9.2 %all_to_all.27 = f32[4,5,8,128]{3,2,1,0:T(8,128)S(1)} all-to-all(f32[4,5,8,128]{3,2,1,0:T(8,128)S(1)} %gram_units.1), channel_id=1, replica_groups=mesh['layer'=8,'zh'=4,'zl'=4,'y'=4] {'zl'}, dimensions={0} | all-to-all | bytes 163840 | tf_op jit(solution)/shard_map/all_to_all | solution.py:346
  42.3 23.0 %all_to_all.28 = f32[4,5,8,128]{3,2,1,0:T(8,128)S(1)} all-to-all(f32[4,5,8,128]{3,2,1,0:T(8,128)S(1)} %broadcast_in_dim.28), channel_id=1, replica_groups=mesh['layer'=8,'zh'=4,'zl'=4,'y'=4] {'zh'}, dimensions={0} | all-to-all | bytes 163840 | tf_op jit(solution)/shard_map/all_to_all | solution.py:348
  65.4 18.9 %all_to_all.29.g_ref = f32[32,5,8,128]{3,2,1,0:T(8,128)S(1)} all-to-all(f32[32,5,8,128]{3,2,1,0:T(8,128)S(1)} %broadcast_in_dim.29), channel_id=1, replica_groups=mesh['layer'=8,'zh'=4,'zl'=4,'y'=4] {'layer','y'}, dimensions={0} | all-to-all | bytes 1310720 | tf_op jit(solution)/shard_map/all_to_all | solution.py:350
  84.3 14.4 %factor_whiten.1 = (f32[8,512]{1,0:T(8,128)}, f32[8,512]{1,0:T(8,128)}) custom-call(s32[1]{0:T(128)} %bitcast.7.shard_ref, f32[32,5,8,128]{3,2,1,0:T(8,128)S(1)} %all_to_all.29.g_ref, f32[8,512]{1,0:T(8,128)S(1)} %get-tuple-element.11.f_ref), custom_call_target="tpu_custom_call" | custom-call | tf_op jit(solution)/shard_map/factor_whiten/pallas_call | solution.py:106
  (5 shorter events, 0.1 us)
Async XLA Ops:
  0.6 31.1 %copy-start = (s32[32,3]{1,0:T(8,128)S(1)}, s32[32,3]{1,0:T(8,128)}, u32[]{:S(2)}) copy-start(s32[32,3]{1,0:T(8,128)} %constant.25.clone.table_ref) | copy-start | bytes 1156

commit v5 on v4

--- a/solution.py
+++ b/solution.py
@@ -27,7 +27,7 @@
     return h,m,l
 def dot_tn(x,y):
     h,m,l=split(x); H,M,L=split(y)
-    p=jnp.concatenate([h,h,m,h,m,l],axis=0); q=jnp.concatenate([H,M,H,L,M,H],axis=0)
+    p=jnp.concatenate([h,h,m],axis=0); q=jnp.concatenate([H,M,H],axis=0)
     return lax.dot_general(p,q,(((0,),(0,)),((),())),preferred_element_type=jnp.float32)
 def factor_block(a_ref, off, u_out, i_out, one):
     n=B//S; per=SUB//S

time: 99.1 us -> 98.9 us (level)
  no operation moved by 1% of the time
where the time goes in v5:
time: 98.9 us; the launch traced here: 98.2 us
  blocking collectives  79.2 us (80%)
  Pallas kernels  18.3 us (19%)
    all_to_all x1, blocking collectives, shards(): lax.all_to_all(jnp.broadcast_to(nearby[None], (far_size,) + nearby.shape)...  23.2 us
    all_to_all x1, blocking collectives, shards(): lax.all_to_all(jnp.broadcast_to(summed[None], (group,) + summed.shape), (...  18.9 us
    all_to_all x1, blocking collectives, shards(): lax.all_to_all(partial.reshape(layers, own_rows, width), 'layer', 0, 0)  15.4 us
    pallas_call x1, Pallas kernels, factor_and_whiten(): pl.pallas_call(functools.partial(factor_kernel, scale), out_shape=(jax.Sh...  14.2 us
    all_to_all x1, blocking collectives, shards(): plane = lax.all_to_all(outgoing, ('layer', 'y'), 0, 0)  12.4 us
    all_to_all x1, blocking collectives, shards(): by_near = lax.all_to_all(packed, 'zl', 0, 0)  9.37 us
    pallas_call x1, Pallas kernels, project(): pl.pallas_call(project_kernel, out_shape=jax.ShapeDtypeStruct((EX_DEV, pr...  2.87 us

profile of v5, /device:TPU:1, one launch (start us, length us, event | category | flops | bytes accessed | tf_op | source)
XLA Modules:
  0.0 98.2 jit_solution(10463264082982350334)
XLA Ops:
  0.6 0.0 copy-start
  0.7 2.9 %project.1 = f32[64,512]{1,0:T(8,128)} custom-call(s32[4,4]{1,0:T(4,128)} %bitcast.13, s32[1,128]{1,0:T(1,128)} %bitcast.14, s32[1,128]{1,0:T(1,128)} %bitcast.15, bf16[8,4096]{1,0:T(8,128)(2,1)} %bitcast.12, bf16[4,512,128]{2,1,0:T(8,128)(2,1)} %bitcast.10, bf16[4096,512]{1,0:T(8,128)(2,1)} %bitcast.9), custom_call_target="tpu_custom_call" | custom-call | tf_op jit(solution)/shard_map/project/pallas_call | solution.py:217
  3.5 15.4 %all_to_all.25.parts_ref = f32[8,8,512]{2,1,0:T(8,128)S(1)} all-to-all(f32[8,8,512]{2,1,0:T(8,128)} %bitcast.11), channel_id=1, replica_groups=mesh['layer'=8,'zh'=4,'zl'=4,'y'=4] {'layer'}, dimensions={0} | all-to-all | bytes 262144 | tf_op jit(solution)/shard_map/all_to_all | solution.py:341
  18.9 12.4 %all_to_all.26.rows_ref = f32[32,2,8,128]{3,2,1,0:T(8,128)S(1)} all-to-all(f32[32,2,8,128]{3,2,1,0:T(8,128)S(1)} %get-tuple-element.10), channel_id=1, replica_groups=mesh['layer'=8,'zh'=4,'zl'=4,'y'=4] {'layer','y'}, dimensions={0} | all-to-all | bytes 524288 | tf_op jit(solution)/shard_map/all_to_all | solution.py:344
  31.3 0.0 copy-done
  31.3 1.2 %gram_units.1 = f32[4,5,8,128]{3,2,1,0:T(8,128)S(1)} custom-call(s32[1]{0:T(128)} %bitcast.6.mine_ref, s32[32,3]{1,0:T(8,128)S(1)} %copy-done, f32[32,2,8,128]{3,2,1,0:T(8,128)S(1)} %all_to_all.26.rows_ref), custom_call_target="tpu_custom_call" | custom-call | tf_op jit(solution)/shard_map/gram_units/pallas_call | solution.py:304
  32.6 9.4 %all_to_all.27 = f32[4,5,8,128]{3,2,1,0:T(8,128)S(1)} all-to-all(f32[4,5,8,128]{3,2,1,0:T(8,128)S(1)} %gram_units.1), channel_id=1, replica_groups=mesh['layer'=8,'zh'=4,'zl'=4,'y'=4] {'zl'}, dimensions={0} | all-to-all | bytes 163840 | tf_op jit(solution)/shard_map/all_to_all | solution.py:346
  42.0 23.2 %all_to_all.28 = f32[4,5,8,128]{3,2,1,0:T(8,128)S(1)} all-to-all(f32[4,5,8,128]{3,2,1,0:T(8,128)S(1)} %broadcast_in_dim.28), channel_id=1, replica_groups=mesh['layer'=8,'zh'=4,'zl'=4,'y'=4] {'zh'}, dimensions={0} | all-to-all | bytes 163840 | tf_op jit(solution)/shard_map/all_to_all | solution.py:348
  65.2 18.9 %all_to_all.29.g_ref = f32[32,5,8,128]{3,2,1,0:T(8,128)S(1)} all-to-all(f32[32,5,8,128]{3,2,1,0:T(8,128)S(1)} %broadcast_in_dim.29), channel_id=1, replica_groups=mesh['layer'=8,'zh'=4,'zl'=4,'y'=4] {'layer','y'}, dimensions={0} | all-to-all | bytes 1310720 | tf_op jit(solution)/shard_map/all_to_all | solution.py:350
  84.1 14.2 %factor_whiten.1 = (f32[8,512]{1,0:T(8,128)}, f32[8,512]{1,0:T(8,128)}) custom-call(s32[1]{0:T(128)} %bitcast.7.shard_ref, f32[32,5,8,128]{3,2,1,0:T(8,128)S(1)} %all_to_all.29.g_ref, f32[8,512]{1,0:T(8,128)S(1)} %get-tuple-element.11.f_ref), custom_call_target="tpu_custom_call" | custom-call | tf_op jit(solution)/shard_map/factor_whiten/pallas_call | solution.py:106
  (5 shorter events, 0.1 us)
Async XLA Ops:
  0.6 30.7 %copy-start = (s32[32,3]{1,0:T(8,128)S(1)}, s32[32,3]{1,0:T(8,128)}, u32[]{:S(2)}) copy-start(s32[32,3]{1,0:T(8,128)} %constant.25.clone.table_ref) | copy-start | bytes 1156
